TPU v7x, 32 devices: a whole 2x2x4 slice. The times are simulated.
32 devices in a mesh: dp: 8 (over y, x, core), shard: 4 (over z).
Axes of the slice: x: 2, y: 2, z: 4, core: 2. Of those that a mesh axis runs over, the one named last changes fastest.
Arguments:
- gradients: bfloat16 [8, 44, 512, 512], P('dp', 'shard'), may hold values from -60 to 60
- owners: int32 [4, 11], P('shard'), may hold values from 0 to 7, as said below
- block_param: int32 [44], replicated, may hold values from 0 to 6, never falling along the last dimension, each value on 1 to 12 neighbouring positions
- left_stat: float32 [16, 4, 512, 512], P('dp', 'shard'), may hold values from -4 to 8, as said below
- right_stat: float32 [16, 4, 512, 512], P('dp', 'shard'), may hold values from -4 to 8, as said below
- moment: float32 [16, 4, 512, 512], P('dp', 'shard'), may hold values from 0.5 to 50
- left_root: bfloat16 [16, 4, 512, 512], P('dp', 'shard'), may hold values from -1 to 3.5, as said below
- right_root: bfloat16 [16, 4, 512, 512], P('dp', 'shard'), may hold values from -1 to 3.5, as said below
Outputs:
- new_left: float32 [16, 4, 512, 512], P('dp', 'shard')
- new_right: float32 [16, 4, 512, 512], P('dp', 'shard')
- new_moment: float32 [16, 4, 512, 512], P('dp', 'shard')
- update: bfloat16 [44, 512, 512], P('shard')
Inputs may be any that keep to these rules, and one draw needn't show every extreme that they name: `owners`: in each row, no value occurs more than 2 times, and some value occurs exactly 2 times. `left_stat`: each slot's matrix is symmetric. `right_stat`: each slot's matrix is symmetric. `left_root`: each slot's matrix is symmetric. `right_root`: each slot's matrix is symmetric.
All inputs are finite; a program needn't handle non-finite values.
Results may differ from a plain program's by a relative error of at most 0.0058.
Values may be sent and summed in bfloat16 or wider, within the bound.
No kernel may reach another device: no remote copies, remote signals or barrier semaphores. Data moves between devices by JAX's collectives and lax.ppermute only.
A program may use at most 192 MiB of HBM per device.

v0:
```python
import jax
import jax.numpy as jnp
from jax import lax
from jax.sharding import PartitionSpec as P

NPARAM = 7
decay_rate = 0.95
tiny_value = 1e-06


def on_device(gradients, owners, block_param, left_stat, right_stat, moment, left_root, right_root):
    replicas = lax.axis_size("dp")
    capacity = left_stat.shape[0]
    blocks = gradients.shape[1]
    block_width = gradients.shape[3]
    device = lax.axis_index("dp")
    column = lax.axis_index("shard")
    owner_row = owners[0]
    counter = jnp.arange(blocks, dtype=jnp.int32)
    same_owner = owner_row[:, None] == owner_row[None, :]
    earlier = counter[None, :] < counter[:, None]
    places = owner_row * capacity + jnp.sum(jnp.where(same_owner & earlier, 1, 0), axis=1).astype(
        jnp.int32
    )
    slot_ids = jnp.arange(replicas * capacity, dtype=jnp.int32)
    matches = places[None, :] == slot_ids[:, None]
    source = jnp.min(jnp.where(matches, counter[None, :], blocks), axis=1)
    partials = gradients[0].astype(jnp.float32)
    row_share = lax.psum_scatter(partials, "dp", scatter_dimension=1, tiled=True)
    share_padded = jnp.concatenate(
        [row_share, jnp.zeros((1,) + row_share.shape[1:], jnp.float32)], axis=0
    )
    outgoing = jnp.take(share_padded, source, axis=0).reshape(
        replicas, capacity, block_width // replicas, block_width
    )
    arrived = lax.all_to_all(outgoing, "dp", split_axis=0, concat_axis=2, tiled=True)
    summed = arrived[0]
    left_gram = jnp.einsum("cij,ckj->cik", summed, summed, precision=lax.Precision.HIGHEST)
    right_gram = jnp.einsum("cji,cjk->cik", summed, summed, precision=lax.Precision.HIGHEST)
    new_left = decay_rate * left_stat + (1.0 - decay_rate) * left_gram[:, None]
    new_right = decay_rate * right_stat + (1.0 - decay_rate) * right_gram[:, None]
    new_moment = decay_rate * moment + (1.0 - decay_rate) * (summed * summed)[:, None]
    adam_step = summed / (jnp.sqrt(new_moment[:, 0]) + tiny_value)
    left_half = jnp.einsum(
        "cij,cjk->cik",
        left_root[:, 0],
        summed.astype(jnp.bfloat16),
        preferred_element_type=jnp.float32,
    ).astype(jnp.bfloat16)
    direction = jnp.einsum(
        "cij,cjk->cik", left_half, right_root[:, 0], preferred_element_type=jnp.float32
    )
    my_slots = lax.dynamic_slice_in_dim(matches, device * capacity, capacity, 0)
    local_params = lax.dynamic_slice_in_dim(block_param, column * blocks, blocks, 0)
    slot_param = jnp.sum(jnp.where(my_slots, local_params[None, :], 0), axis=1)
    is_live = jnp.any(my_slots, axis=1)
    param_ids = jnp.arange(NPARAM, dtype=jnp.int32)
    member = (slot_param[:, None] == param_ids[None, :]) & is_live[:, None]
    adam_squares = jnp.sum(adam_step * adam_step, axis=(1, 2))
    direction_squares = jnp.sum(direction * direction, axis=(1, 2))
    adam_local = jnp.sum(jnp.where(member, adam_squares[:, None], 0.0), axis=0)
    direction_local = jnp.sum(jnp.where(member, direction_squares[:, None], 0.0), axis=0)
    adam_norm, direction_norm = lax.psum((adam_local, direction_local), ("dp", "shard"))
    graft_ratio = jnp.sqrt((adam_norm + tiny_value) / (direction_norm + tiny_value))
    slot_ratio = jnp.sum(jnp.where(member, graft_ratio[None, :], 0.0), axis=1)
    slot_update = (slot_ratio[:, None, None] * direction).astype(jnp.bfloat16)
    gathered = lax.all_gather(slot_update, "dp", axis=0, tiled=True)
    update = jnp.take(gathered, places, axis=0)
    return (new_left, new_right, new_moment, update)


def solution(mesh):
    return jax.shard_map(
        on_device,
        mesh=mesh,
        in_specs=(
            P("dp", "shard", None, None),
            P("shard", None),
            P(),
            P("dp", "shard", None, None),
            P("dp", "shard", None, None),
            P("dp", "shard", None, None),
            P("dp", "shard", None, None),
            P("dp", "shard", None, None),
        ),
        out_specs=(
            P("dp", "shard", None, None),
            P("dp", "shard", None, None),
            P("dp", "shard", None, None),
            P("shard", None, None),
        ),
        check_vma=False,
    )
```

profile of v0, /device:TPU:0, one launch (start us, length us, event | category | flops | bytes accessed | tf_op | source)
XLA Modules:
  0.0 273.2 jit_solution(2395701479978908789)
XLA Ops:
  7.2 8.7 %bitcast_convert_fusion = f32[11,512,512]{2,1,0:T(8,128)} fusion(bf16[1,11,512,512]{3,2,1,0:T(8,128)(2,1)} %param.8), kind=kLoop, calls=%fused_computation.2 | loop fusion | flops 2883584 | bytes 17301504 | tf_op jit(solution)/shard_map/convert_element_type | solution.py:28
  15.9 0.6 copy-done.6
  17.0 88.7 %reduce-scatter.2.cloned.1.call-done = f32[11,64,512]{2,1,0:T(8,128)} async-done(((f32[11,512,512]{2,1,0:T(8,128)}), f32[11,64,512]{2,1,0:T(8,128)}) %reduce-scatter.2.cloned.1.call-update) | async-done | bytes 1441808 | tf_op jit(solution)/shard_map/reduce_scatter | solution.py:29
  105.6 1.5 concatenate.3
  107.2 2.0 gather_fusion
  109.2 3.3 %broadcast_select_fusion.1 = f32[8,2,64,512]{3,2,1,0:T(8,128)} fusion(f32[8,2,64,512]{3,2,1,0:T(8,128)} %bitcast.79, pred[8,2]{1,0:T(8,128)(4,1)S(1)} %compare_and_fusion), kind=kLoop, calls=%fused_computation.24 | loop fusion | flops 524288 | bytes 4194320 | tf_op jit(solution)/shard_map/jit(_take)/select_n | solution.py:33
  112.5 3.7 %all-to-all-start = ((f32[8,2,64,512]{3,2,1,0:T(8,128)}), f32[8,2,64,512]{3,2,1,0:T(8,128)S(1)}, u32[]{:S(2)}, u32[]{:S(2)}) async-start(f32[8,2,64,512]{3,2,1,0:T(8,128)} %broadcast_select_fusion.1), calls=%async_computation.1 | async-start | bytes 4194304 | tf_op jit(solution)/shard_map/all_to_all | solution.py:36
  116.6 26.2 %all-to-all-done = f32[8,2,64,512]{3,2,1,0:T(8,128)S(1)} async-done(((f32[8,2,64,512]{3,2,1,0:T(8,128)}), f32[8,2,64,512]{3,2,1,0:T(8,128)S(1)}, u32[]{:S(2)}, u32[]{:S(2)}) %all-to-all-start) | async-done | bytes 2097184 | tf_op jit(solution)/shard_map/all_to_all | solution.py:36
  142.8 0.3 multiply_multiply_fusion
  143.1 1.1 copy-done.2
  144.1 0.2 copy.47
  144.3 2.0 copy.43
  146.3 0.2 copy-done.3
  146.6 2.8 %sqrt_add_fusion = (f32[2,1,512,512]{3,2,0,1:T(8,128)}, f32[2,1,512,512]{3,2,0,1:T(8,128)}) fusion(f32[1,2,8,64,512]{4,3,2,1,0:T(8,128)S(1)} %copy.47, f32[2,1,512,512]{3,2,1,0:T(8,128)S(1)} %copy-done.3), kind=kLoop, calls=%fused_computation.16 | loop fusion | flops 1572864 | bytes 8388608 | tf_op jit(solution)/shard_map/add | solution.py:43
  149.3 4.0 %multiply_reduce_fusion = (f32[2]{0:T(128)S(1)}, f32[2,512,512]{2,1,0:T(8,128)}) fusion(bf16[2,1,512,512]{3,2,1,0:T(8,128)(2,1)S(1)} %copy-done, bf16[2,1,512,512]{3,2,1,0:T(8,128)(2,1)} %param.14, f32[2,512,512]{2,1,0:T(8,128)S(1)} %bitcast.75), kind=kOutput, calls=%fused_computation.15 | convolution fusion | flops 1075838976 | bytes 6291464 | tf_op jit(solution)/shard_map/cij,cjk->cik/dot_general | solution.py:50
  153.3 2.7 fusion.3
  156.1 39.5 %all-reduce.1 = (f32[7]{0:T(128)S(1)}, f32[7]{0:T(128)S(1)}) all-reduce(f32[7]{0:T(128)S(1)} %get-tuple-element.21, f32[7]{0:T(128)S(1)} %get-tuple-element.20), channel_id=1, replica_groups=mesh['dp'=8,'shard'=4] {'dp','shard'}, use_global_device_ids=true, to_apply=%region_10.11 | all-reduce | flops 14 | bytes 112 | tf_op jit(solution)/shard_map/psum | solution.py:63
  195.5 0.2 select_reduce_fusion.2
  195.7 3.0 %multiply_convert_fusion = bf16[2,512,512]{2,1,0:T(8,128)(2,1)} fusion(f32[2,512,512]{2,1,0:T(8,128)} %get-tuple-element.27, f32[2]{0:T(128)S(1)} %select_reduce_fusion.2), kind=kLoop, calls=%fused_computation.14 | loop fusion | flops 1048576 | bytes 3145736 | tf_op jit(solution)/shard_map/convert_element_type | solution.py:66
  198.8 6.1 %fusion = f32[2,1,512,512]{3,2,1,0:T(8,128)} fusion(f32[2,1,512,512]{3,2,1,0:T(8,128)} %param.12, f32[2,512,512]{2,1,0:T(8,128)S(1)} %bitcast.76), kind=kOutput, calls=%fused_computation.7 | convolution fusion | flops 3222798336 | bytes 6291456 | tf_op jit(solution)/shard_map/cji,cjk->cik/dot_general | solution.py:39
  204.9 5.0 %fusion.1 = f32[2,1,512,512]{3,2,1,0:T(8,128)} fusion(f32[2,1,512,512]{3,2,1,0:T(8,128)S(1)} %copy-done.4, f32[2,512,512]{2,1,0:T(8,128)S(1)} %bitcast.77), kind=kOutput, calls=%fused_computation.10 | convolution fusion | flops 3222798336 | bytes 6291456 | tf_op jit(solution)/shard_map/cij,ckj->cik/dot_general | solution.py:38
  209.9 43.1 %all-gather.2.cloned.1.call-done = bf16[16,512,512]{2,1,0:T(8,128)(2,1)} async-done(((bf16[2,512,512]{2,1,0:T(8,128)(2,1)}), bf16[16,512,512]{2,1,0:T(8,128)(2,1)}) %all-gather.2.cloned.1.call-update) | async-done | bytes 8388624 | tf_op jit(solution)/shard_map/all_gather | solution.py:67
  253.0 7.4 %gather_fusion.1 = bf16[11,512,512]{2,1,0:T(8,128)(2,1)} fusion(bf16[16,512,512]{2,1,0:T(8,128)(2,1)} %all-gather.2.cloned.1.call-done, s32[1024]{0:T(1024)S(1)} %pad_clamp_fusion), kind=kCustom, calls=%fused_computation.1 | custom fusion | bytes 11534380 | tf_op jit(solution)/shard_map/jit(_take)/gather | solution.py:68
  260.5 5.9 %broadcast_select_fusion = bf16[11,512,512]{2,1,0:T(8,128)(2,1)} fusion(bf16[11,512,512]{2,1,0:T(8,128)(2,1)} %gather_fusion.1, pred[11]{0:T(512)(128)(4,1)S(1)} %compare_and_fusion.2), kind=kLoop, calls=%fused_computation.3 | loop fusion | flops 2883584 | bytes 11534347 | tf_op jit(solution)/shard_map/jit(_take)/select_n | solution.py:68
  (31 shorter events, 1.0 us)
Async XLA Ops:
  7.2 142.2 %copy-start = (bf16[2,1,512,512]{3,2,1,0:T(8,128)(2,1)S(1)}, bf16[2,1,512,512]{3,2,1,0:T(8,128)(2,1)}, u32[]{:S(2)}) copy-start(bf16[2,1,512,512]{3,2,1,0:T(8,128)(2,1)} %param.15) | copy-start | bytes 3145732
  7.2 98.5 %reduce-scatter.2.cloned.1.call-start = ((), (), s32[]{:S(2)}) async-start(), calls=%async_computation.2 | async-start | bytes 12976128 | tf_op jit(solution)/shard_map/reduce_scatter | solution.py:29
  15.9 0.7 copy-start.6
  112.5 3.8 %copy-start.5 = (s32[44]{0:T(128)S(1)}, s32[44]{0:T(128)}, u32[]{:S(2)}) copy-start(s32[44]{0:T(128)} %param.10) | copy-start | bytes 532
  112.5 30.3 %all-to-all-start = ((f32[8,2,64,512]{3,2,1,0:T(8,128)}), f32[8,2,64,512]{3,2,1,0:T(8,128)S(1)}, u32[]{:S(2)}, u32[]{:S(2)}) async-start(f32[8,2,64,512]{3,2,1,0:T(8,128)} %broadcast_select_fusion.1), calls=%async_computation.1 | async-start | bytes 4194304 | tf_op jit(solution)/shard_map/all_to_all | solution.py:36
  116.2 136.8 %all-gather.2.cloned.1.call-start = ((), (), s32[]{:S(2)}) async-start(), calls=%async_computation.3 | async-start | bytes 9437184 | tf_op jit(solution)/shard_map/all_gather | solution.py:67
  142.8 1.3 copy-start.2
  144.3 2.2 copy-start.3
  198.8 6.2 %copy-start.4 = (f32[2,1,512,512]{3,2,1,0:T(8,128)S(1)}, f32[2,1,512,512]{3,2,1,0:T(8,128)}, u32[]{:S(2)}) copy-start(f32[2,1,512,512]{3,2,1,0:T(8,128)} %param.11) | copy-start | bytes 6291460
  260.5 5.9 %copy-start.1 = (bf16[2,1,512,512]{3,2,1,0:T(8,128)(2,1)S(1)}, bf16[2,1,512,512]{3,2,1,0:T(8,128)(2,1)}, u32[]{:S(2)}) copy-start(bf16[2,1,512,512]{3,2,1,0:T(8,128)(2,1)} %param.15) | copy-start | bytes 3145732
Sparse Core Ops, SparseCore 0:
  16.0 89.5 reduce-scatter.1
  198.9 54.1 all-gather.1
where the time goes:
time: 274 us; the launch traced here: 273 us
  waiting for transfers between devices  158 us (58%)
  blocking collectives  39.5 us (14%)
  other arithmetic  27.4 us (10%)
  local copies, waits for them, and re-layouts  15.3 us (6%)
  matrix products  15.1 us (6%)
  between operations  14.2 us (5%)
  starting transfers between devices  3.82 us (1%)
    reduce_scatter x1, waiting for transfers between devices, on_device(): lax.psum_scatter(partials, 'dp', scatter_dimension=1, tiled=True)  88.7 us
    all_gather x1, waiting for transfers between devices, on_device(): gathered = lax.all_gather(slot_update, 'dp', axis=0, tiled=True)  43.1 us
    psum x1, blocking collectives, on_device(): lax.psum((adam_local, direction_local), ('dp', 'shard'))  39.5 us
    all_to_all x1, waiting for transfers between devices, on_device(): lax.all_to_all(outgoing, 'dp', split_axis=0, concat_axis=2, tiled=True)  26.2 us
    convert_element_type x1, other arithmetic, on_device(): partials = gradients[0].astype(jnp.float32)  8.67 us
    gather x1, local copies, waits for them, and re-layouts, on_device(): update = jnp.take(gathered, places, axis=0)  7.44 us
    dot_general x1, matrix products, on_device(): jnp.einsum('cji,cjk->cik', summed, summed, precision=lax.Precision.HIGHEST)  6.14 us
    select_n x2, other arithmetic, on_device(): update = jnp.take(gathered, places, axis=0)  5.87 us
  transfers between devices with their start and end apart: 3, of which 3 were waited for; matrix products, arithmetic and copies ran while one was open for 4% of the time, Pallas kernels for 0%

commit v1 on v0

--- a/solution.py
+++ b/solution.py
@@ -6,6 +6,22 @@
 NPARAM = 7
 decay_rate = 0.95
 tiny_value = 1e-06
+
+
+def exchange_in_pairs(x, axis, split, join):
+    ways, here = (lax.axis_size(axis), lax.axis_index(axis))
+    width = x.shape[split] // ways
+    shape = list(x.shape)
+    shape[split] = width
+    height = shape[join]
+    shape[join] = height * ways
+    full = jnp.zeros(shape, x.dtype)
+    for mask in range(ways):
+        part = lax.dynamic_slice_in_dim(x, (here ^ mask) * width, width, axis=split)
+        if mask:
+            part = lax.ppermute(part, axis, [(d, d ^ mask) for d in range(ways)])
+        full = lax.dynamic_update_slice_in_dim(full, part, (here ^ mask) * height, axis=join)
+    return full
 
 
 def on_device(gradients, owners, block_param, left_stat, right_stat, moment, left_root, right_root):
@@ -33,7 +49,7 @@
     outgoing = jnp.take(share_padded, source, axis=0).reshape(
         replicas, capacity, block_width // replicas, block_width
     )
-    arrived = lax.all_to_all(outgoing, "dp", split_axis=0, concat_axis=2, tiled=True)
+    arrived = exchange_in_pairs(outgoing, "dp", 0, 2)
     summed = arrived[0]
     left_gram = jnp.einsum("cij,ckj->cik", summed, summed, precision=lax.Precision.HIGHEST)
     right_gram = jnp.einsum("cji,cjk->cik", summed, summed, precision=lax.Precision.HIGHEST)

time: 274 us -> 265 us (0.967)
  waiting for transfers between devices: 158 us -> 150 us
    all_to_all x1 -> x0, waiting for transfers between devices: 26.2 us -> none  [on_device(): lax.all_to_all(outgoing, 'dp', split_axis=0, concat_axis=2, tiled=True)]
    ppermute x0 -> x7, waiting for transfers between devices: none -> 20.1 us  [exchange_in_pairs(): part = lax.ppermute(part, axis, [(d, d ^ mask) for d in range(ways)])]
    ppermute x0 -> x7, starting transfers between devices: none -> 5.19 us  [exchange_in_pairs(): part = lax.ppermute(part, axis, [(d, d ^ mask) for d in range(ways)])]
    all_to_all x1 -> x0, starting transfers between devices: 3.74 us -> none  [on_device(): lax.all_to_all(outgoing, 'dp', split_axis=0, concat_axis=2, tiled=True)]
    unnamed x0 -> x1, other arithmetic: none -> 3.58 us
    add x1 -> x0, other arithmetic: 2.78 us -> none  [on_device(): adam_step = summed / (jnp.sqrt(new_moment[:, 0]) + tiny_value)]
  transfers between devices with their start and end apart: 3 -> 9, of which waited for: 3 -> 5; matrix products, arithmetic and copies ran while one was open for 4% -> 6% of each run, Pallas kernels for 0% -> 0%
where the time goes in v1:
time: 265 us; the launch traced here: 264 us
  waiting for transfers between devices  150 us (57%)
  blocking collectives  39.5 us (15%)
  other arithmetic  25 us (9%)
  local copies, waits for them, and re-layouts  15.8 us (6%)
  between operations  14.4 us (5%)
  matrix products  14 us (5%)
  starting transfers between devices  5.27 us (2%)
    reduce_scatter x1, waiting for transfers between devices, on_device(): lax.psum_scatter(partials, 'dp', scatter_dimension=1, tiled=True)  88.7 us
    all_gather x1, waiting for transfers between devices, on_device(): gathered = lax.all_gather(slot_update, 'dp', axis=0, tiled=True)  41.5 us
    psum x1, blocking collectives, on_device(): lax.psum((adam_local, direction_local), ('dp', 'shard'))  39.5 us
    ppermute x7, waiting for transfers between devices, exchange_in_pairs(): part = lax.ppermute(part, axis, [(d, d ^ mask) for d in range(ways)])  20.1 us
    convert_element_type x1, other arithmetic, on_device(): partials = gradients[0].astype(jnp.float32)  8.67 us
    gather x1, local copies, waits for them, and re-layouts, on_device(): update = jnp.take(gathered, places, axis=0)  7.44 us
    select_n x2, other arithmetic, on_device(): update = jnp.take(gathered, places, axis=0)  5.87 us
  transfers between devices with their start and end apart: 9, of which 5 were waited for; matrix products, arithmetic and copies ran while one was open for 6% of the time, Pallas kernels for 0%

profile of v1, /device:TPU:0, one launch (start us, length us, event | category | flops | bytes accessed | tf_op | source)
XLA Modules:
  0.0 264.3 jit_solution(6561988839351269895)
XLA Ops:
  7.2 8.7 %bitcast_convert_fusion = f32[11,512,512]{2,1,0:T(8,128)} fusion(bf16[1,11,512,512]{3,2,1,0:T(8,128)(2,1)} %param.8), kind=kLoop, calls=%fused_computation.2 | loop fusion | flops 2883584 | bytes 17301504 | tf_op jit(solution)/shard_map/convert_element_type | solution.py:44
  17.0 88.7 %reduce-scatter.2.cloned.1.call-done = f32[11,64,512]{2,1,0:T(8,128)} async-done(((f32[11,512,512]{2,1,0:T(8,128)}), f32[11,64,512]{2,1,0:T(8,128)}) %reduce-scatter.2.cloned.1.call-update) | async-done | bytes 1441808 | tf_op jit(solution)/shard_map/reduce_scatter | solution.py:45
  105.6 1.5 concatenate.3
  107.2 2.0 gather_fusion
  109.2 1.9 broadcast_select_fusion.1
  111.1 1.3 copy-done.3
  112.4 1.2 constant_dynamic-slice_fusion.1
  114.1 1.5 collective-permute-start.1
  116.0 1.5 collective-permute-start.3
  117.9 1.1 bitcast_dynamic-update-slice_fusion.7
  119.1 1.5 collective-permute-start.5
  120.6 2.9 %collective-permute-done.1 = f32[1,2,64,512]{3,2,1,0:T(8,128)S(1)} collective-permute-done((f32[1,2,64,512]{3,2,1,0:T(8,128)}, f32[1,2,64,512]{3,2,1,0:T(8,128)S(1)}, u32[]{:S(2)}, u32[]{:S(2)}) %collective-permute-start.1) | collective-permute-done | bytes 262176 | tf_op jit(solution)/shard_map/ppermute | solution.py:22
  123.7 4.6 %collective-permute-done.2 = f32[1,2,64,512]{3,2,1,0:T(8,128)S(1)} collective-permute-done((f32[1,2,64,512]{3,2,1,0:T(8,128)}, f32[1,2,64,512]{3,2,1,0:T(8,128)S(1)}, u32[]{:S(2)}, u32[]{:S(2)}) %collective-permute-start.2) | collective-permute-done | bytes 262176 | tf_op jit(solution)/shard_map/ppermute | solution.py:22
  128.4 12.6 %collective-permute-done.4 = f32[1,2,64,512]{3,2,1,0:T(8,128)S(1)} collective-permute-done((f32[1,2,64,512]{3,2,1,0:T(8,128)}, f32[1,2,64,512]{3,2,1,0:T(8,128)S(1)}, u32[]{:S(2)}, u32[]{:S(2)}) %collective-permute-start.4) | collective-permute-done | bytes 262176 | tf_op jit(solution)/shard_map/ppermute | solution.py:22
  141.1 1.2 fusion.3
  142.3 4.0 %multiply_reduce_fusion = (f32[2]{0:T(128)S(1)}, f32[2,512,512]{2,1,0:T(8,128)}) fusion(bf16[2,1,512,512]{3,2,1,0:T(8,128)(2,1)S(1)} %copy-done, bf16[2,1,512,512]{3,2,1,0:T(8,128)(2,1)} %param.14, f32[2,512,512]{2,1,0:T(8,128)S(1)} %bitcast_dynamic-update-slice_fusion), kind=kOutput, calls=%fused_computation.15 | convolution fusion | flops 1075838976 | bytes 6291464 | tf_op jit(solution)/shard_map/cij,cjk->cik/dot_general | solution.py:66
  146.4 39.5 %all-reduce.1 = (f32[7]{0:T(128)S(1)}, f32[7]{0:T(128)S(1)}) all-reduce(f32[7]{0:T(128)S(1)} %get-tuple-element.21, f32[7]{0:T(128)S(1)} %get-tuple-element.20), channel_id=1, replica_groups=mesh['dp'=8,'shard'=4] {'dp','shard'}, use_global_device_ids=true, to_apply=%region_10.11 | all-reduce | flops 14 | bytes 112 | tf_op jit(solution)/shard_map/psum | solution.py:79
  186.1 2.9 %multiply_convert_fusion = bf16[2,512,512]{2,1,0:T(8,128)(2,1)} fusion(f32[2,512,512]{2,1,0:T(8,128)} %get-tuple-element.32, f32[2]{0:T(128)S(1)} %select_reduce_fusion.2), kind=kLoop, calls=%fused_computation.14 | loop fusion | flops 1048576 | bytes 3145736 | tf_op jit(solution)/shard_map/convert_element_type | solution.py:82
  189.0 3.6 %fusion.4 = f32[2,1,512,512]{3,2,1,0:T(8,128)} fusion(f32[2,512,512]{2,1,0:T(8,128)S(1)} %bitcast_dynamic-update-slice_fusion, f32[2,1,512,512]{3,2,1,0:T(8,128)} %param.13), kind=kLoop, calls=%fused_computation.17 | loop fusion | flops 2097152 | bytes 6291456
  192.6 5.0 %fusion.1 = f32[2,1,512,512]{3,2,1,0:T(8,128)} fusion(f32[2,1,512,512]{3,2,1,0:T(8,128)S(1)} %copy-done.4, f32[2,512,512]{2,1,0:T(8,128)S(1)} %bitcast_dynamic-update-slice_fusion), kind=kOutput, calls=%fused_computation.9 | convolution fusion | flops 3222798336 | bytes 6291456 | tf_op jit(solution)/shard_map/cji,cjk->cik/dot_general | solution.py:55
  197.6 5.0 %fusion.2 = f32[2,1,512,512]{3,2,1,0:T(8,128)} fusion(f32[2,1,512,512]{3,2,1,0:T(8,128)S(1)} %copy-done.5, f32[2,512,512]{2,1,0:T(8,128)S(1)} %bitcast_dynamic-update-slice_fusion), kind=kOutput, calls=%fused_computation.12 | convolution fusion | flops 3222798336 | bytes 6291456 | tf_op jit(solution)/shard_map/cij,ckj->cik/dot_general | solution.py:54
  202.6 41.5 %all-gather.2.cloned.1.call-done = bf16[16,512,512]{2,1,0:T(8,128)(2,1)} async-done(((bf16[2,512,512]{2,1,0:T(8,128)(2,1)}), bf16[16,512,512]{2,1,0:T(8,128)(2,1)}) %all-gather.2.cloned.1.call-update) | async-done | bytes 8388624 | tf_op jit(solution)/shard_map/all_gather | solution.py:83
  244.1 7.4 %gather_fusion.1 = bf16[11,512,512]{2,1,0:T(8,128)(2,1)} fusion(bf16[16,512,512]{2,1,0:T(8,128)(2,1)} %all-gather.2.cloned.1.call-done, s32[1024]{0:T(1024)S(1)} %pad_clamp_fusion), kind=kCustom, calls=%fused_computation.1 | custom fusion | bytes 11534380 | tf_op jit(solution)/shard_map/jit(_take)/gather | solution.py:84
  251.6 5.9 %broadcast_select_fusion = bf16[11,512,512]{2,1,0:T(8,128)(2,1)} fusion(bf16[11,512,512]{2,1,0:T(8,128)(2,1)} %gather_fusion.1, pred[11]{0:T(512)(128)(4,1)S(1)} %compare_and_fusion.2), kind=kLoop, calls=%fused_computation.3 | loop fusion | flops 2883584 | bytes 11534347 | tf_op jit(solution)/shard_map/jit(_take)/select_n | solution.py:84
  (56 shorter events, 2.8 us)
Async XLA Ops:
  7.2 135.1 %copy-start = (bf16[2,1,512,512]{3,2,1,0:T(8,128)(2,1)S(1)}, bf16[2,1,512,512]{3,2,1,0:T(8,128)(2,1)}, u32[]{:S(2)}) copy-start(bf16[2,1,512,512]{3,2,1,0:T(8,128)(2,1)} %param.15) | copy-start | bytes 3145732
  7.2 98.5 %reduce-scatter.2.cloned.1.call-start = ((), (), s32[]{:S(2)}) async-start(), calls=%async_computation.1 | async-start | bytes 12976128 | tf_op jit(solution)/shard_map/reduce_scatter | solution.py:45
  15.9 0.7 copy-start.9
  15.9 228.2 %all-gather.2.cloned.1.call-start = ((), (), s32[]{:S(2)}) async-start(), calls=%async_computation.2 | async-start | bytes 9437184 | tf_op jit(solution)/shard_map/all_gather | solution.py:83
  111.1 1.3 copy-start.3
  112.4 1.3 copy-start.8
  113.7 5.4 %collective-permute-start = (f32[1,2,64,512]{3,2,1,0:T(8,128)}, f32[1,2,64,512]{3,2,1,0:T(8,128)S(1)}, u32[]{:S(2)}, u32[]{:S(2)}) collective-permute-start(f32[1,2,64,512]{3,2,1,0:T(8,128)} %get-tuple-element.30), channel_id=1, source_target_pairs={{0,4},{4,0},{8,12},{12,8},{16,20},{20,16},{24,28},{28,24},{1,5},{5... | collective-permute-start | bytes 786440 | tf_op jit(solution)/shard_map/ppermute | solution.py:22
  113.8 5.3 %copy-start.7 = (f32[1,2,64,512]{3,2,1,0:T(8,128)S(1)}, f32[1,2,64,512]{3,2,1,0:T(8,128)}, u32[]{:S(2)}) copy-start(f32[1,2,64,512]{3,2,1,0:T(8,128)} %get-tuple-element.25) | copy-start | bytes 786436
  113.8 9.8 %copy-start.6 = (f32[1,2,64,512]{3,2,1,0:T(8,128)S(1)}, f32[1,2,64,512]{3,2,1,0:T(8,128)}, u32[]{:S(2)}) copy-start(f32[1,2,64,512]{3,2,1,0:T(8,128)} %get-tuple-element.24) | copy-start | bytes 786436
  114.1 9.5 %collective-permute-start.1 = (f32[1,2,64,512]{3,2,1,0:T(8,128)}, f32[1,2,64,512]{3,2,1,0:T(8,128)S(1)}, u32[]{:S(2)}, u32[]{:S(2)}) collective-permute-start(f32[1,2,64,512]{3,2,1,0:T(8,128)} %get-tuple-element.29), channel_id=1, source_target_pairs={{0,8},{4,12},{8,0},{12,4},{16,24},{20,28},{24,16},{28,20},{1,9},{5... | collective-permute-start | bytes 786440 | tf_op jit(solution)/shard_map/ppermute | solution.py:22
  115.7 12.6 %collective-permute-start.2 = (f32[1,2,64,512]{3,2,1,0:T(8,128)}, f32[1,2,64,512]{3,2,1,0:T(8,128)S(1)}, u32[]{:S(2)}, u32[]{:S(2)}) collective-permute-start(f32[1,2,64,512]{3,2,1,0:T(8,128)} %get-tuple-element.28), channel_id=1, source_target_pairs={{0,12},{4,8},{8,4},{12,0},{16,28},{20,24},{24,20},{28,16},{1,13},{... | collective-permute-start | bytes 786440 | tf_op jit(solution)/shard_map/ppermute | solution.py:22
  116.0 12.4 %collective-permute-start.3 = (f32[1,2,64,512]{3,2,1,0:T(8,128)}, f32[1,2,64,512]{3,2,1,0:T(8,128)S(1)}, u32[]{:S(2)}, u32[]{:S(2)}) collective-permute-start(f32[1,2,64,512]{3,2,1,0:T(8,128)} %get-tuple-element.27), channel_id=1, source_target_pairs={{0,16},{4,20},{8,24},{12,28},{16,0},{20,4},{24,8},{28,12},{1,17},{... | collective-permute-start | bytes 786440 | tf_op jit(solution)/shard_map/ppermute | solution.py:22
  117.5 23.5 %collective-permute-start.4 = (f32[1,2,64,512]{3,2,1,0:T(8,128)}, f32[1,2,64,512]{3,2,1,0:T(8,128)S(1)}, u32[]{:S(2)}, u32[]{:S(2)}) collective-permute-start(f32[1,2,64,512]{3,2,1,0:T(8,128)} %get-tuple-element.26), channel_id=1, source_target_pairs={{0,20},{4,16},{8,28},{12,24},{16,4},{20,0},{24,12},{28,8},{1,21},{... | collective-permute-start | bytes 786440 | tf_op jit(solution)/shard_map/ppermute | solution.py:22
  117.9 23.2 %copy-start.2 = (f32[2,1,512,512]{3,2,1,0:T(8,128)S(1)}, f32[2,1,512,512]{3,2,1,0:T(8,128)}, u32[]{:S(2)}) copy-start(f32[2,1,512,512]{3,2,1,0:T(8,128)} %param.13) | copy-start | bytes 6291460
  119.1 21.9 %collective-permute-start.5 = (f32[1,2,64,512]{3,2,1,0:T(8,128)S(1)}, f32[1,2,64,512]{3,2,1,0:T(8,128)S(1)}, u32[]{:S(2)}, u32[]{:S(2)}) collective-permute-start(f32[1,2,64,512]{3,2,1,0:T(8,128)S(1)} %copy-done.7), channel_id=1, source_target_pairs={{0,24},{4,28},{8,16},{12,20},{16,8},{20,12},{24,0},{28,4},{1,25},{... | collective-permute-start | bytes 786440 | tf_op jit(solution)/shard_map/ppermute | solution.py:22
  123.6 17.5 %collective-permute-start.6 = (f32[1,2,64,512]{3,2,1,0:T(8,128)S(1)}, f32[1,2,64,512]{3,2,1,0:T(8,128)S(1)}, u32[]{:S(2)}, u32[]{:S(2)}) collective-permute-start(f32[1,2,64,512]{3,2,1,0:T(8,128)S(1)} %copy-done.6), channel_id=1, source_target_pairs={{0,28},{4,24},{8,20},{12,16},{16,12},{20,8},{24,4},{28,0},{1,29},{... | collective-permute-start | bytes 786440 | tf_op jit(solution)/shard_map/ppermute | solution.py:22
  189.0 3.6 %copy-start.4 = (f32[2,1,512,512]{3,2,1,0:T(8,128)S(1)}, f32[2,1,512,512]{3,2,1,0:T(8,128)}, u32[]{:S(2)}) copy-start(f32[2,1,512,512]{3,2,1,0:T(8,128)} %param.12) | copy-start | bytes 6291460
  192.6 5.0 %copy-start.5 = (f32[2,1,512,512]{3,2,1,0:T(8,128)S(1)}, f32[2,1,512,512]{3,2,1,0:T(8,128)}, u32[]{:S(2)}) copy-start(f32[2,1,512,512]{3,2,1,0:T(8,128)} %param.11) | copy-start | bytes 6291460
  251.6 5.9 %copy-start.1 = (bf16[2,1,512,512]{3,2,1,0:T(8,128)(2,1)S(1)}, bf16[2,1,512,512]{3,2,1,0:T(8,128)(2,1)}, u32[]{:S(2)}) copy-start(bf16[2,1,512,512]{3,2,1,0:T(8,128)(2,1)} %param.15) | copy-start | bytes 3145732
Sparse Core Ops, SparseCore 0:
  16.0 89.5 reduce-scatter.1
  189.1 54.9 all-gather.1
